TPU v7x, 256 devices: a whole 4x4x8 slice. The times are simulated.
256 devices in a mesh: leaf: 64 (over z, x, core), group: 4 (over y).
Axes of the slice: x: 4, y: 4, z: 8, core: 2. Of those that a mesh axis runs over, the one named last changes fastest.
Arguments:
- q_two: float32 [524288, 256], P(('group', 'leaf'))
- q_one: float32 [524288, 256], P(('group', 'leaf'))
- sources: float32 [524288, 256], P(('group', 'leaf'))
- coupling_two: float32 [2, 256, 256], replicated, as said below
- coupling_one: float32 [256, 256], replicated, as said below
Outputs:
- panel_one: float32 [524288, 256], P(('group', 'leaf'))
- solution: float32 [524288, 256], P(('group', 'leaf'))
Inputs may be any that keep to these rules, and one draw needn't show every extreme that they name: coupling_two[0], coupling_two[1] and coupling_one are symmetric and positive definite. `coupling_one`: symmetric and positive definite.
All inputs are finite; a program needn't handle non-finite values.
Results may differ from a plain program's by a relative error of at most 0.00019.
Values sent between devices are 32-bit elements; how exact they have to be, the bound alone decides.
A program may use at most 64 MiB of HBM per device.

v0:
```python
import jax
import jax.numpy as jnp
from jax import lax
from jax.sharding import PartitionSpec as P

HIGH = lax.Precision.HIGHEST


def from_partner(block, axis, distance):
    count = lax.axis_size(axis)
    route = []
    for low in range(count):
        high = low | 1 << distance
        if high != low and high < count:
            route += [(low, high), (high, low)]
    return lax.ppermute(block, axis, route)


def gram_of(left, right):
    return lax.dot_general(
        left, right, (((0,), (0,)), ((), ())), precision=HIGH, preferred_element_type=jnp.float32
    )


def times_matrix(left, right):
    return jnp.dot(left, right, precision=HIGH, preferred_element_type=jnp.float32)


def definite_solve(matrix, target):
    factor = jnp.linalg.cholesky(matrix)
    lower_part = lax.linalg.triangular_solve(factor, target, left_side=True, lower=True)
    return lax.linalg.triangular_solve(
        factor, lower_part, left_side=True, lower=True, transpose_a=True
    )


def half_sums(local_terms):
    summed = lax.psum(local_terms, "leaf")
    return summed + from_partner(summed, "group", 0)


def per_device(q_two, q_one, sources, coupling_two, coupling_one):
    panel_width = q_two.shape[1]
    half_index = lax.axis_index("group") // 2
    coupling = lax.dynamic_index_in_dim(coupling_two, half_index, 0, keepdims=False)
    level_terms = [gram_of(q_two, q_two), gram_of(q_two, q_one), gram_of(q_two, sources)]
    summed = half_sums(jnp.concatenate(level_terms, axis=1))
    gram_two = summed[:, :panel_width]
    cross = summed[:, panel_width : 2 * panel_width]
    projected = summed[:, 2 * panel_width : 3 * panel_width]
    solved = definite_solve(coupling + gram_two, jnp.concatenate([cross, projected], axis=1))
    update = times_matrix(q_two, solved)
    panel_one = q_one - update[:, :panel_width]
    level_field = sources - update[:, panel_width:]
    top_terms = jnp.concatenate([gram_of(q_one, panel_one), gram_of(q_one, level_field)], axis=1)
    totals = lax.psum(top_terms, ("leaf", "group"))
    weights = definite_solve(coupling_one + totals[:, :panel_width], totals[:, panel_width:])
    solution = level_field - times_matrix(panel_one, weights)
    return (panel_one, solution)


def solution(mesh):
    placed = (
        P(("group", "leaf"), None),
        P(("group", "leaf"), None),
        P(("group", "leaf"), None),
        P(),
        P(),
    )
    return jax.shard_map(
        per_device,
        mesh=mesh,
        in_specs=placed,
        out_specs=(P(("group", "leaf"), None), P(("group", "leaf"), None)),
        check_vma=False,
    )
```

profile of v0, /device:TPU:1, one launch (start us, length us, event | category | flops | bytes accessed | tf_op | source)
XLA Modules:
  0.0 649.1 jit_solution(9518811791308798356)
XLA Ops:
  8.8 3.4 fusion.33
  12.2 3.6 fusion.34
  15.9 3.6 fusion.35
  20.5 187.5 %all-reduce.4.cloned.1.call-done = f32[256,768]{0,1:T(8,128)} async-done(((f32[256,768]{0,1:T(8,128)}), f32[256,768]{0,1:T(8,128)}) %all-reduce.4.cloned.1.call-update) | async-done | bytes 786448 | tf_op jit(solution)/shard_map/psum | solution.py:38
  209.5 2.9 copy.10
  212.4 2.9 copy.9
  215.5 9.9 %collective-permute-done = f32[256,768]{0,1:T(8,128)} collective-permute-done((f32[256,768]{0,1:T(8,128)}, f32[256,768]{0,1:T(8,128)}, u32[]{:S(2)}, u32[]{:S(2)}) %collective-permute-start) | collective-permute-done | bytes 786464 | tf_op jit(solution)/shard_map/ppermute | solution.py:16
  227.8 11.7 %cholesky.130 = f32[128,128]{1,0:T(8,128)S(1)} custom-call(f32[128,128]{1,0:T(8,128)S(1)} %cholesky.194), custom_call_target="Cholesky" | custom-call | tf_op jit(solution)/shard_map/jit(cholesky)/cholesky | solution.py:30
  239.6 9.8 %custom-call.21 = f32[1,128,128]{1,2,0:T(8,128)S(1)} custom-call(f32[1,128,128]{2,1,0:T(8,128)S(1)} %get-tuple-element.48), custom_call_target="InvertDiagBlocksLowerTriangular" | custom-call | tf_op jit(solution)/shard_map/jit(cholesky)/cholesky | solution.py:30
  251.6 11.7 %cholesky.147 = f32[128,128]{1,0:T(8,128)S(1)} custom-call(f32[128,128]{1,0:T(8,128)S(1)} %convolution_subtract_fusion.5), custom_call_target="Cholesky" | custom-call | tf_op jit(solution)/shard_map/jit(cholesky)/cholesky | solution.py:30
  265.4 4.0 while.2
  269.4 28.4 %custom-call.18 = f32[2,128,128]{1,2,0:T(8,128)S(1)} custom-call(f32[2,128,128]{2,1,0:T(8,128)S(1)} %get-tuple-element.10), custom_call_target="InvertDiagBlocksLowerTriangular" | custom-call | tf_op jit(solution)/shard_map/triangular_solve | solution.py:32
  300.5 7.0 %convolution_bitcast_fusion = f32[2048,512]{0,1:T(8,128)S(1)} fusion(f32[2048,256]{1,0:T(8,128)S(1)} %copy-done, f32[128,512]{1,0:T(8,128)S(1)} %fusion.20, f32[128,512]{1,0:T(8,128)S(1)} %fusion.19), kind=kOutput, calls=%fused_computation.4 | convolution fusion | flops 3221356544 | bytes 6815744 | tf_op jit(solution)/shard_map/dot_general | solution.py:26
  307.5 2.0 convolution_bitcast_fusion.1
  311.0 2.1 convolution_bitcast_fusion.2
  314.1 2.9 copy.14
  317.0 252.6 %all-reduce.6.cloned.1.call-done = f32[256,512]{0,1:T(8,128)} async-done(((f32[256,512]{0,1:T(8,128)}), f32[256,512]{0,1:T(8,128)}) %all-reduce.6.cloned.1.call-update) | async-done | bytes 524304 | tf_op jit(solution)/shard_map/psum | solution.py:56
  570.8 11.7 %cholesky.164 = f32[128,128]{1,0:T(8,128)S(1)} custom-call(f32[128,128]{1,0:T(8,128)S(1)} %cholesky.197), custom_call_target="Cholesky" | custom-call | tf_op jit(solution)/shard_map/jit(cholesky)/cholesky | solution.py:30
  582.6 9.8 %custom-call.22 = f32[1,128,128]{1,2,0:T(8,128)S(1)} custom-call(f32[1,128,128]{2,1,0:T(8,128)S(1)} %get-tuple-element.44), custom_call_target="InvertDiagBlocksLowerTriangular" | custom-call | tf_op jit(solution)/shard_map/jit(cholesky)/cholesky | solution.py:30
  592.9 11.7 %cholesky.181 = f32[128,128]{1,0:T(8,128)S(1)} custom-call(f32[128,128]{1,0:T(8,128)S(1)} %convolution_subtract_fusion.4), custom_call_target="Cholesky" | custom-call | tf_op jit(solution)/shard_map/jit(cholesky)/cholesky | solution.py:30
  607.3 4.0 while.3
  611.4 19.9 %custom-call.19 = f32[2,128,128]{1,2,0:T(8,128)S(1)} custom-call(f32[2,128,128]{2,1,0:T(8,128)S(1)} %get-tuple-element.18), custom_call_target="InvertDiagBlocksLowerTriangular" | custom-call | tf_op jit(solution)/shard_map/triangular_solve | solution.py:32
  633.2 5.7 convolution_subtract_fusion
  638.9 2.9 copy.15
  (89 shorter events, 27.5 us)
Async XLA Ops:
  7.2 1.6 copy-start
  7.2 200.8 %all-reduce.4.cloned.1.call-start = ((), (), s32[]{:S(2)}) async-start(), calls=%async_computation | async-start | bytes 1572864 | tf_op jit(solution)/shard_map/psum | solution.py:38
  8.8 3.5 copy-start.1
  12.2 3.7 copy-start.8
  20.5 549.2 %all-reduce.6.cloned.1.call-start = ((), (), s32[]{:S(2)}) async-start(), calls=%async_computation.1 | async-start | bytes 1048576 | tf_op jit(solution)/shard_map/psum | solution.py:56
  208.0 17.4 %collective-permute-start = (f32[256,768]{0,1:T(8,128)}, f32[256,768]{0,1:T(8,128)}, u32[]{:S(2)}, u32[]{:S(2)}) collective-permute-start(f32[256,768]{0,1:T(8,128)} %all-reduce.4.cloned.1.call-done), channel_id=1, source_target_pairs={{0,1},{1,0},{2,3},{3,2},{4,5},{5,4},{6,7},{7,6},{8,9},{9,8},{10,11... | collective-permute-start | bytes 2359304 | tf_op jit(solution)/shard_map/ppermute | solution.py:16
  212.4 2.9 copy-start.12
  227.1 0.7 copy-start.9
  300.4 7.0 %copy-start.2 = (f32[2048,256]{1,0:T(8,128)S(1)}, f32[2048,256]{1,0:T(8,128)}, u32[]{:S(2)}) copy-start(f32[2048,256]{1,0:T(8,128)} %param.7) | copy-start | bytes 6291460
  300.5 7.0 %copy-start.6 = (f32[2048,256]{0,1:T(8,128)S(1)}, f32[2048,256]{0,1:T(8,128)}, u32[]{:S(2)}) copy-start(f32[2048,256]{0,1:T(8,128)} %copy.10) | copy-start | bytes 6291460
  307.5 2.1 copy-start.5
  307.5 3.1 copy-start.7
  311.0 2.2 copy-start.3
  311.0 3.0 copy-start.11
  570.6 60.7 %copy-start.10 = (f32[256,512]{0,1:T(8,128)S(1)}, f32[256,512]{0,1:T(8,128)}, u32[]{:S(2)}) copy-start(f32[256,512]{0,1:T(8,128)} %all-reduce.6.cloned.1.call-done) | copy-start | bytes 1572868
  631.3 1.9 copy-start.4
Sparse Core Ops, SparseCore 0:
  20.6 187.3 all-reduce.3
  314.1 255.5 all-reduce.5
where the time goes:
time: 658 us; the launch traced here: 649 us
  waiting for transfers between devices  450 us (68%)
  other arithmetic  122 us (19%)
  matrix products  34.6 us (5%)
  local copies, waits for them, and re-layouts  23.6 us (4%)
  between operations  17.5 us (3%)
    psum x1, waiting for transfers between devices, per_device(): totals = lax.psum(top_terms, ('leaf', 'group'))  253 us
    psum x1, waiting for transfers between devices, half_sums(): summed = lax.psum(local_terms, 'leaf')  187 us
    another operation x13, other arithmetic, definite_solve(): factor = jnp.linalg.cholesky(matrix)  68.6 us
    another operation x5, other arithmetic, definite_solve(): lax.linalg.triangular_solve(factor, lower_part, left_side=True, lower=Tru...  48.4 us
    unnamed x33, local copies, waits for them, and re-layouts  15.2 us
    dot_general x5, matrix products, gram_of(): lax.dot_general(left, right, (((0,), (0,)), ((), ())), precision=HIGH, pr...  14.8 us
  transfers between devices with their start and end apart: 3, of which 3 were waited for; matrix products, arithmetic and copies ran while one was open for 1% of the time, Pallas kernels for 0%

commit v1 on v0

v1 whole, which is shorter than its diff:
```python
import functools
import jax
import jax.numpy as jnp
from jax import lax
from jax.experimental import pallas as pl
from jax.experimental.pallas import tpu as pltpu
from jax.sharding import PartitionSpec as P

HIGH = lax.Precision.HIGHEST
F32 = jnp.float32
B = 16
N = 256
HALF = 128
NC, NX, NZ, NY = 2, 4, 8, 4
PAIRED = 3
STREAMS = 5


def split(value):
    top = value.astype(jnp.bfloat16)
    rest = (value - top.astype(F32)).astype(jnp.bfloat16)
    return top, rest


def dot3(left, right):
    out = jnp.dot(left[0], right[1], preferred_element_type=F32)
    out = out + jnp.dot(left[1], right[0], preferred_element_type=F32)
    return out + jnp.dot(left[0], right[0], preferred_element_type=F32)


def dot3t(left, right):
    dims = (((0,), (0,)), ((), ()))
    out = lax.dot_general(left[0], right[1], dims, preferred_element_type=F32)
    out = out + lax.dot_general(left[1], right[0], dims, preferred_element_type=F32)
    return out + lax.dot_general(left[0], right[0], dims, preferred_element_type=F32)


def gram_kernel(two_ref, one_ref, src_ref, out_ref):
    step = pl.program_id(0)
    two, one, src = split(two_ref[...]), split(one_ref[...]), split(src_ref[...])
    right = [two, one, src]
    for pos, (left, item) in enumerate([(two, two), (two, one), (two, src), (one, one), (one, src)]):
        block = dot3t(left, item)
        for side in range(2):
            part = block[:, side * HALF : (side + 1) * HALF]
            spot = pl.ds(side * N, N)

            @pl.when(step == 0)
            def _():
                out_ref[pos, spot, :] = part

            @pl.when(step > 0)
            def _():
                out_ref[pos, spot, :] += part


def gram_call(q_two, q_one, sources, tile):
    rows = q_two.shape[0]
    spec = pl.BlockSpec((tile, N), lambda i: (i, 0))
    return pl.pallas_call(
        gram_kernel,
        grid=(rows // tile,),
        in_specs=[spec, spec, spec],
        out_specs=pl.BlockSpec((STREAMS, 2 * N, HALF), lambda i: (0, 0, 0)),
        out_shape=jax.ShapeDtypeStruct((STREAMS, 2 * N, HALF), F32),
    )(q_two, q_one, sources)


def here():
    leaf = lax.axis_index("leaf")
    return leaf % NC, (leaf // NC) % NX, leaf // (NC * NX), lax.axis_index("group")


def place(core, x, z, y):
    return {"leaf": (z * NX + x) * NC + core, "group": y}


def neighbours():
    core, x, z, y = here()
    found = [place(1 - core, x, z, y)]
    found += [place(core, (x + d) % NX, z, y) for d in range(1, NX)]
    found += [place(core, x, (z + d) % NZ, y) for d in range(1, NZ)]
    found += [place(core, x, z, (y + d) % NY) for d in range(1, NY)]
    return found


def greet():
    barrier = pltpu.get_barrier_semaphore()
    peers = neighbours()
    for peer in peers:
        pl.semaphore_signal(barrier, inc=1, device_id=peer, device_id_type=pl.DeviceIdType.MESH)
    pl.semaphore_wait(barrier, len(peers))


def stream(pos, g_ref, out_ref, out_pos, core_buf, x_buf, z_buf, y_buf, a1, a2, a3, send, recv):
    core, x, z, y = here()
    paired = pos < PAIRED
    started = []
    count = [0]

    def copy(src, dst, peer):
        slot = count[0]
        count[0] += 1
        item = pltpu.make_async_remote_copy(
            src_ref=src, dst_ref=dst, send_sem=send.at[pos, slot], recv_sem=recv.at[pos, slot],
            device_id=peer, device_id_type=pl.DeviceIdType.MESH)
        item.start()
        started.append(item)
        return item

    mate = place(1 - core, x, z, y)
    first = copy(g_ref.at[pos, pl.ds((1 - core) * 256, 256), :], core_buf.at[pos], mate)
    yield
    first.wait_recv()
    a1[pos] = g_ref[pos, pl.ds(core * 256, 256), :] + core_buf[pos]
    wave = []
    for d in range(1, NX):
        to = (x + d) % NX
        wave.append(copy(a1.at[pos, pl.ds(to * 64, 64), :], x_buf.at[pos, d - 1], place(core, to, z, y)))
    yield
    for item in wave:
        item.wait_recv()
    a2[pos] = (a1[pos, pl.ds(x * 64, 64), :] + x_buf[pos, 1]) + (x_buf[pos, 0] + x_buf[pos, 2])
    wave = []
    for d in range(1, NZ):
        to = (z + d) % NZ
        wave.append(copy(a2.at[pos, pl.ds(to * 8, 8), :], z_buf.at[pos, d - 1], place(core, x, to, y)))
    yield
    for item in wave:
        item.wait_recv()
    total = a2[pos, pl.ds(z * 8, 8), :]
    for d in range(1, NZ):
        total = total + z_buf[pos, d - 1]
    a3[pos] = total
    wave = []
    for d in range(1, NY):
        to = (y + d) % NY
        wave.append(copy(a3.at[pos], y_buf.at[pos, y], place(core, x, z, to)))
    yield
    for item in wave:
        item.wait_recv()
    parts = []
    for q in range(NY):
        parts.append(jnp.where(y == q, total, y_buf[pos, q]))
    spot = core * 256 + x * 64 + z * 8
    if paired:
        out_ref[out_pos, 0, pl.ds(spot, 8), :] = parts[0] + parts[1]
        out_ref[out_pos, 1, pl.ds(spot, 8), :] = parts[2] + parts[3]
    else:
        out_ref[out_pos, pl.ds(spot, 8), :] = (parts[0] + parts[1]) + (parts[2] + parts[3])

    def window(start, size):
        if paired:
            return out_ref.at[out_pos, :, pl.ds(start, size), :]
        return out_ref.at[out_pos, pl.ds(start, size), :]

    wave = []
    for d in range(1, NZ):
        to = (z + d) % NZ
        wave.append(copy(window(spot, 8), window(spot, 8), place(core, x, to, y)))
    yield
    for item in wave:
        item.wait_recv()
    spot = core * 256 + x * 64
    wave = []
    for d in range(1, NX):
        to = (x + d) % NX
        wave.append(copy(window(spot, 64), window(spot, 64), place(core, to, z, y)))
    yield
    for item in wave:
        item.wait_recv()
    spot = core * 256
    last = copy(window(spot, 256), window(spot, 256), mate)
    yield
    last.wait_recv()
    yield
    for item in started:
        item.wait_send()


COPIES = 1 + (NX - 1) + (NZ - 1) + (NY - 1) + (NZ - 1) + (NX - 1) + 1


def reduce_kernel(g_ref, pair_ref, total_ref, *scratch):
    greet()
    lines = []
    for pos in range(STREAMS):
        out_ref, out_pos = (pair_ref, pos) if pos < PAIRED else (total_ref, pos - PAIRED)
        lines.append(stream(pos, g_ref, out_ref, out_pos, *scratch))
    alive = []
    while lines or alive:
        if lines:
            alive.append(lines.pop(0))
        alive = [item for item in alive if next(item, "end") != "end"]


def reduce_call(g):
    vmem = pl.BlockSpec(memory_space=pltpu.VMEM)
    return pl.pallas_call(
        reduce_kernel,
        in_specs=[vmem],
        out_specs=[vmem, vmem],
        out_shape=[
            jax.ShapeDtypeStruct((PAIRED, 2, 2 * N, HALF), F32),
            jax.ShapeDtypeStruct((STREAMS - PAIRED, 2 * N, HALF), F32),
        ],
        scratch_shapes=[
            pltpu.VMEM((STREAMS, 256, HALF), F32),
            pltpu.VMEM((STREAMS, NX - 1, 64, HALF), F32),
            pltpu.VMEM((STREAMS, NZ - 1, 8, HALF), F32),
            pltpu.VMEM((STREAMS, NY, 8, HALF), F32),
            pltpu.VMEM((STREAMS, 256, HALF), F32),
            pltpu.VMEM((STREAMS, 64, HALF), F32),
            pltpu.VMEM((STREAMS, 8, HALF), F32),
            pltpu.SemaphoreType.DMA((STREAMS, COPIES)),
            pltpu.SemaphoreType.DMA((STREAMS, COPIES)),
        ],
        compiler_params=pltpu.CompilerParams(collective_id=0, has_side_effects=True),
    )(g)


def mm(a, b):
    return jnp.dot(a, b, precision=HIGH, preferred_element_type=F32)

def mmt(a, b):
    return lax.dot_general(a, b, (((0,), (0,)), ((), ())), precision=HIGH, preferred_element_type=F32)

def eliminate(rows, base):
    lane = lax.broadcasted_iota(jnp.int32, (B, 128), 1)
    sub = lax.broadcasted_iota(jnp.int32, (B, 128), 0)
    cols = [jnp.broadcast_to(rows[:, base + j : base + j + 1], (B, 128)) for j in range(B)]
    inside = (lane >= base) & (lane < base + B)
    body = jnp.where(inside, jnp.where(lane - base == sub, 1.0, 0.0), rows)
    for k in range(B):
        here = sub == k
        inv = 1.0 / cols[k][k : k + 1, :]
        col = jnp.where(here, -1.0, cols[k])
        for j in range(k + 1, B):
            t = cols[j][k : k + 1, :] * inv
            cols[j] = jnp.where(here, 0.0, cols[j]) - col * t
        t = body[k : k + 1, :] * inv
        body = jnp.where(here, 0.0, body) - col * t
    return body

def invert(refs):
    lane = lax.broadcasted_iota(jnp.int32, (128, 128), 1)
    sub = lax.broadcasted_iota(jnp.int32, (128, 128), 0)
    nblk = 128 // B
    heads = [r[0:B, :] for r in refs]
    for p in range(nblk):
        base = p * B
        in_lane = (lane >= base) & (lane < base + B)
        in_sub = (sub >= base) & (sub < base + B)
        outs = [eliminate(h, base) for h in heads]
        for m, ref in enumerate(refs):
            a = ref[...]
            r = outs[m]
            if p + 1 < nblk:
                nxt = a[base + B : base + 2 * B, :]
                acc = jnp.where(in_lane[:B], 0.0, nxt)
                for j in range(B):
                    acc = acc - jnp.broadcast_to(nxt[:, base + j : base + j + 1], (B, 128)) * r[j : j + 1, :]
                heads[m] = acc
            left = jnp.where(in_lane, jnp.where(in_sub, jnp.where(lane == sub, -1.0, 0.0), a), 0.0)
            parts = []
            if p > 0:
                parts.append(jnp.zeros((base, 128), F32))
            parts.append(r)
            if p + 1 < nblk:
                parts.append(jnp.zeros((128 - base - B, 128), F32))
            right = jnp.concatenate(parts, axis=0) if len(parts) > 1 else r
            ref[...] = jnp.where(in_lane | in_sub, 0.0, a) - mm(left, right)

def solve_all(k_list, z_list, work):
    n = len(k_list)
    for i in range(n):
        work[i][...] = k_list[i][0:128, 0:128]
    invert(work[:n])
    t, zt, z2 = [], [], []
    for i in range(n):
        i1 = work[i][...]
        k12 = k_list[i][0:128, 128:256]
        tk = mm(i1, k12)
        tz = mm(i1, z_list[i][0:128, :])
        z2.append(z_list[i][128:256, :] - mmt(k12, tz))
        t.append(tk); zt.append(tz)
        work[i][...] = k_list[i][128:256, 128:256] - mmt(k12, tk)
    invert(work[:n])
    out = []
    for i in range(n):
        s2 = mm(work[i][...], z2[i])
        s1 = zt[i] - mm(t[i], s2)
        out.append(jnp.concatenate([s1, s2], axis=0))
    return out


def whole(ref, *lead):
    return jnp.concatenate([ref[(*lead, slice(0, N))], ref[(*lead, slice(N, 2 * N))]], axis=1)


def solve_kernel(pair_ref, total_ref, couple_two_ref, couple_one_ref, top_ref, rest_ref, *work):
    half = lax.axis_index("group") // 2
    matrices, targets, crosses = [], [], []
    for h in range(2):
        matrices.append(couple_two_ref[h] + whole(pair_ref, 0, h))
        crosses.append(whole(pair_ref, 1, h))
        targets.append(jnp.concatenate([crosses[h], whole(pair_ref, 2, h)], axis=1))
    solved = solve_all(matrices, targets, work)
    lower = jnp.concatenate([whole(total_ref, 0) + couple_one_ref[...], whole(total_ref, 1)], axis=1)
    for h in range(2):
        lower = lower - mmt(crosses[h], solved[h])
    weights = solve_all([lower[:, :N]], [lower[:, N:]], work)[0]
    mine = jnp.where(half == 0, solved[0], solved[1])
    field = mine[:, N:] - mm(mine[:, :N], weights)
    for pos, item in enumerate([mine[:, :N], field, weights]):
        top, rest = split(item)
        top_ref[:, pos * N : (pos + 1) * N] = top
        rest_ref[:, pos * N : (pos + 1) * N] = rest


def solve_call(pair, total, couple_two, couple_one):
    vmem = pl.BlockSpec(memory_space=pltpu.VMEM)
    shape = jax.ShapeDtypeStruct((N, 3 * N), jnp.bfloat16)
    return pl.pallas_call(
        solve_kernel,
        in_specs=[vmem] * 4,
        out_specs=[vmem, vmem],
        out_shape=[shape, shape],
        scratch_shapes=[pltpu.VMEM((HALF, HALF), F32)] * 2,
    )(pair, total, couple_two, couple_one)


def update_kernel(two_ref, one_ref, src_ref, top_ref, rest_ref, panel_ref, sol_ref):
    two, one = split(two_ref[...]), split(one_ref[...])
    top, rest = top_ref[...], rest_ref[...]
    wide = dot3(two, (top[:, : 2 * N], rest[:, : 2 * N]))
    panel_ref[...] = one_ref[...] - wide[:, :N]
    sol_ref[...] = src_ref[...] - wide[:, N:] - dot3(one, (top[:, 2 * N :], rest[:, 2 * N :]))


def update_call(q_two, q_one, sources, top, rest, tile):
    rows = q_two.shape[0]
    spec = pl.BlockSpec((tile, N), lambda i: (i, 0))
    full = pl.BlockSpec((N, 3 * N), lambda i: (0, 0))
    shape = jax.ShapeDtypeStruct((rows, N), F32)
    return pl.pallas_call(
        update_kernel,
        grid=(rows // tile,),
        in_specs=[spec, spec, spec, full, full],
        out_specs=[spec, spec],
        out_shape=[shape, shape],
    )(q_two, q_one, sources, top, rest)


def per_device(q_two, q_one, sources, coupling_two, coupling_one):
    g = gram_call(q_two, q_one, sources, 512)
    pair, total = reduce_call(g)
    top, rest = solve_call(pair, total, coupling_two, coupling_one)
    panel_one, result = update_call(q_two, q_one, sources, top, rest, 256)
    return (panel_one, result)


def solution(mesh):
    placed = (
        P(("group", "leaf"), None),
        P(("group", "leaf"), None),
        P(("group", "leaf"), None),
        P(),
        P(),
    )
    return jax.shard_map(
        per_device,
        mesh=mesh,
        in_specs=placed,
        out_specs=(P(("group", "leaf"), None), P(("group", "leaf"), None)),
        check_vma=False,
    )
```

time: 658 us -> 104 us (0.16); the launches traced: 649 us -> 104 us
  waiting for transfers between devices: 450 us -> 0 us
  other arithmetic: 122 us -> 0 us
  Pallas kernels: 0 us -> 103 us
  matrix products: 34.6 us -> 0 us
  local copies, waits for them, and re-layouts: 23.6 us -> 0 us
  between operations: 17.5 us -> 0.64 us
    psum x2 -> x0, waiting for transfers between devices: 440 us -> none  [the longest x1 253 us: per_device(): totals = lax.psum(top_terms, ('leaf', 'group'))]
    another operation x18 -> x0, other arithmetic: 117 us -> none  [the longest x13 68.6 us: definite_solve(): factor = jnp.linalg.cholesky(matrix)]
    pallas_call x0 -> x4, Pallas kernels: none -> 103 us  [the longest x1 59.9 us: reduce_call(): pl.pallas_call(reduce_kernel, in_specs=[vmem], out_specs=[vmem, vmem], ou...]
    dot_general x7 -> x0, matrix products: 27.5 us -> none  [the longest x5 14.8 us: gram_of(): lax.dot_general(left, right, (((0,), (0,)), ((), ())), precision=HIGH, pr...]
    unnamed x33 -> x0, local copies, waits for them, and re-layouts: 15.2 us -> none
    ppermute x1 -> x0, waiting for transfers between devices: 9.91 us -> none  [from_partner(): return lax.ppermute(block, axis, route)]
    another operation x17 -> x0, local copies, waits for them, and re-layouts: 8.02 us -> none
    another operation x16 -> x0, matrix products: 7.07 us -> none  [the longest x4 2.63 us: definite_solve(): factor = jnp.linalg.cholesky(matrix)]
  transfers between devices with their start and end apart: 3 -> 0, of which waited for: 3 -> 0; matrix products, arithmetic and copies ran while one was open for 1% -> 0% of each run, Pallas kernels for 0% -> 0%
where the time goes in v1:
time: 104 us
  Pallas kernels  103 us (99%)
    pallas_call x1, Pallas kernels, reduce_call(): pl.pallas_call(reduce_kernel, in_specs=[vmem], out_specs=[vmem, vmem], ou...  59.9 us
    pallas_call x1, Pallas kernels, solve_call(): pl.pallas_call(solve_kernel, in_specs=[vmem] * 4, out_specs=[vmem, vmem],...  20.4 us
    pallas_call x1, Pallas kernels, gram_call(): pl.pallas_call(gram_kernel, grid=(rows // tile,), in_specs=[spec, spec, s...  14.3 us
    pallas_call x1, Pallas kernels, update_call(): pl.pallas_call(update_kernel, grid=(rows // tile,), in_specs=[spec, spec,...  8.49 us

profile of v1, /device:TPU:1, one launch (start us, length us, event | category | flops | bytes accessed | tf_op | source)
XLA Modules:
  0.0 103.8 jit_solution(17600835936649099854)
XLA Ops:
  0.6 14.3 %shard_map.68.g_ref = f32[5,512,128]{2,1,0:T(8,128)} custom-call(f32[2048,256]{1,0:T(8,128)} %two_ref.3, f32[2048,256]{1,0:T(8,128)} %one_ref.3, f32[2048,256]{1,0:T(8,128)} %src_ref.3), custom_call_target="tpu_custom_call" | custom-call | tf_op jit(solution)/shard_map/pallas_call | solution.py:60
  15.0 59.9 %shard_map.69 = (f32[3,2,512,128]{3,2,1,0:T(8,128)}, f32[2,512,128]{2,1,0:T(8,128)}) custom-call(f32[5,512,128]{2,1,0:T(8,128)} %shard_map.68.g_ref), custom_call_target="tpu_custom_call" | custom-call | tf_op jit(solution)/shard_map/pallas_call | solution.py:199
  74.9 20.4 %shard_map.70 = (bf16[256,768]{1,0:T(8,128)(2,1)}, bf16[256,768]{1,0:T(8,128)(2,1)}) custom-call(f32[3,2,512,128]{3,2,1,0:T(8,128)} %get-tuple-element.6.pair_ref, f32[2,512,128]{2,1,0:T(8,128)} %get-tuple-element.7.total_ref, f32[2,256,256]{2,1,0:T(8,128)} %couple_two_ref.1, f32[256,256]{1,0:T(8,128)} %couple_one_ref.1), custom_call_target="tpu_custom_call" | custom-call | tf_op jit(solution)/shard_map/pallas_call | solution.py:324
  95.3 8.5 %shard_map.71 = (f32[2048,256]{1,0:T(8,128)}, f32[2048,256]{1,0:T(8,128)}) custom-call(f32[2048,256]{1,0:T(8,128)} %two_ref.3, f32[2048,256]{1,0:T(8,128)} %one_ref.3, f32[2048,256]{1,0:T(8,128)} %src_ref.3, bf16[256,768]{1,0:T(8,128)(2,1)} %get-tuple-element.8.top_ref, bf16[256,768]{1,0:T(8,128)(2,1)} %get-tuple-element.9.rest_ref), custom_call_target="tpu_custom_call" | custom-call | tf_op jit(solution)/shard_map/pallas_call | solution.py:346

commit v2 on v1

v2 whole, which is shorter than its diff:
```python
import jax
import jax.numpy as jnp
from jax import lax
from jax.experimental import pallas as pl
from jax.experimental.pallas import tpu as pltpu
from jax.sharding import PartitionSpec as P

HIGH = lax.Precision.HIGHEST
F32 = jnp.float32
B = 16
N = 256
HALF = 128
NC, NX, NZ, NY = 2, 4, 8, 4
PAIRED = 3
STREAMS = 5
PHASES = 10
COPIES = 1 + 4 + 2 + (NZ - 1) + (NY - 1) + (NZ - 1) + 2 + 2 + 1


def split(value):
    top = value.astype(jnp.bfloat16)
    rest = (value - top.astype(F32)).astype(jnp.bfloat16)
    return top, rest


def dot3(left, right):
    out = jnp.dot(left[0], right[1], preferred_element_type=F32)
    out = out + jnp.dot(left[1], right[0], preferred_element_type=F32)
    return out + jnp.dot(left[0], right[0], preferred_element_type=F32)


def dot3t(left, right):
    dims = (((0,), (0,)), ((), ()))
    out = lax.dot_general(left[0], right[1], dims, preferred_element_type=F32)
    out = out + lax.dot_general(left[1], right[0], dims, preferred_element_type=F32)
    return out + lax.dot_general(left[0], right[0], dims, preferred_element_type=F32)


def here():
    leaf = lax.axis_index("leaf")
    return leaf % NC, (leaf // NC) % NX, leaf // (NC * NX), lax.axis_index("group")


def place(core, x, z, y):
    return {"leaf": (z * NX + x) * NC + core, "group": y}


def neighbours():
    core, x, z, y = here()
    found = [place(1 - core, x, z, y), place(core, x + 1 - 2 * (x % 2), z, y), place(core, 3 - x, z, y)]
    found += [place(core, x, (z + d) % NZ, y) for d in range(1, NZ)]
    found += [place(core, x, z, (y + d) % NY) for d in range(1, NY)]
    return found


def stream(pos, g_ref, out_ref, out_pos, core_buf, x_buf, mid_buf, last_buf, z_buf, y_buf, a1, a2, a3, send, recv):
    core, x, z, y = here()
    paired = pos < PAIRED
    near, far, across = x + 1 - 2 * (x % 2), 3 - x, (x + 2) % NX
    started = []
    count = [0]

    def copy(src, dst, peer):
        slot = count[0]
        count[0] += 1
        item = pltpu.make_async_remote_copy(
            src_ref=src, dst_ref=dst, send_sem=send.at[pos, slot], recv_sem=recv.at[pos, slot],
            device_id=peer, device_id_type=pl.DeviceIdType.MESH)
        item.start()
        started.append(item)
        return item

    mate = place(1 - core, x, z, y)
    peers = [place(core, near, z, y), place(core, far, z, y)]
    chunks = [near, far]
    first = copy(g_ref.at[pos, pl.ds((1 - core) * 256, 256), :], core_buf.at[pos], mate)
    yield
    first.wait_recv()
    a1[pos] = g_ref[pos, pl.ds(core * 256, 256), :] + core_buf[pos]
    wave = []
    for sub in range(2):
        wave.append(copy(a1.at[pos, pl.ds(across * 64 + sub * 32, 32), :], x_buf.at[pos, sub, 1], peers[sub]))
        wave.append(copy(a1.at[pos, pl.ds(chunks[sub] * 64 + sub * 32, 32), :], x_buf.at[pos, sub, 0], peers[sub]))
    yield
    for item in wave:
        item.wait_recv()
    wave = []
    for sub in range(2):
        mid_buf[pos, sub] = a1[pos, pl.ds(chunks[1 - sub] * 64 + sub * 32, 32), :] + x_buf[pos, sub, 1]
        wave.append(copy(mid_buf.at[pos, sub], last_buf.at[pos, sub], peers[1 - sub]))
    yield
    for sub in range(2):
        wave[sub].wait_recv()
        a2[pos, pl.ds(sub * 32, 32), :] = (
            a1[pos, pl.ds(x * 64 + sub * 32, 32), :] + x_buf[pos, sub, 0] + last_buf[pos, sub])
    wave = []
    for d in range(1, NZ):
        to = (z + d) % NZ
        wave.append(copy(a2.at[pos, pl.ds(to * 8, 8), :], z_buf.at[pos, d - 1], place(core, x, to, y)))
    yield
    for item in wave:
        item.wait_recv()
    total = a2[pos, pl.ds(z * 8, 8), :]
    for d in range(1, NZ):
        total = total + z_buf[pos, d - 1]
    a3[pos] = total
    wave = []
    for d in range(1, NY):
        to = (y + d) % NY
        wave.append(copy(a3.at[pos], y_buf.at[pos, y], place(core, x, z, to)))
    yield
    for item in wave:
        item.wait_recv()
    parts = []
    for q in range(NY):
        parts.append(jnp.where(y == q, a3[pos], y_buf[pos, q]))
    spot = core * 256 + x * 64 + z * 8
    if paired:
        out_ref[out_pos, 0, pl.ds(spot, 8), :] = parts[0] + parts[1]
        out_ref[out_pos, 1, pl.ds(spot, 8), :] = parts[2] + parts[3]
    else:
        out_ref[out_pos, pl.ds(spot, 8), :] = (parts[0] + parts[1]) + (parts[2] + parts[3])

    def window(start, size):
        if paired:
            return out_ref.at[out_pos, :, pl.ds(start, size), :]
        return out_ref.at[out_pos, pl.ds(start, size), :]

    wave = []
    for d in range(1, NZ):
        to = (z + d) % NZ
        wave.append(copy(window(spot, 8), window(spot, 8), place(core, x, to, y)))
    yield
    for item in wave:
        item.wait_recv()
    spot = core * 256 + x * 64
    wave = [copy(window(spot, 64), window(spot, 64), peers[side]) for side in range(2)]
    yield
    for item in wave:
        item.wait_recv()
    wave = []
    for side in range(2):
        spot = core * 256 + chunks[side] * 64 + side * 32
        wave.append(copy(window(spot, 32), window(spot, 32), peers[1 - side]))
    yield
    for item in wave:
        item.wait_recv()
    spot = core * 256
    last = copy(window(spot, 256), window(spot, 256), mate)
    yield
    last.wait_recv()
    yield
    for item in started:
        item.wait_send()


def mm(a, b):
    return jnp.dot(a, b, precision=HIGH, preferred_element_type=F32)

def mmt(a, b):
    return lax.dot_general(a, b, (((0,), (0,)), ((), ())), precision=HIGH, preferred_element_type=F32)

def eliminate(rows, base):
    lane = lax.broadcasted_iota(jnp.int32, (B, 128), 1)
    sub = lax.broadcasted_iota(jnp.int32, (B, 128), 0)
    cols = [jnp.broadcast_to(rows[:, base + j : base + j + 1], (B, 128)) for j in range(B)]
    inside = (lane >= base) & (lane < base + B)
    body = jnp.where(inside, jnp.where(lane - base == sub, 1.0, 0.0), rows)
    for k in range(B):
        here = sub == k
        inv = 1.0 / cols[k][k : k + 1, :]
        col = jnp.where(here, -1.0, cols[k])
        for j in range(k + 1, B):
            t = cols[j][k : k + 1, :] * inv
            cols[j] = jnp.where(here, 0.0, cols[j]) - col * t
        t = body[k : k + 1, :] * inv
        body = jnp.where(here, 0.0, body) - col * t
    return body

def invert(refs):
    lane = lax.broadcasted_iota(jnp.int32, (128, 128), 1)
    sub = lax.broadcasted_iota(jnp.int32, (128, 128), 0)
    nblk = 128 // B
    heads = [r[0:B, :] for r in refs]
    for p in range(nblk):
        base = p * B
        in_lane = (lane >= base) & (lane < base + B)
        in_sub = (sub >= base) & (sub < base + B)
        outs = [eliminate(h, base) for h in heads]
        for m, ref in enumerate(refs):
            a = ref[...]
            r = outs[m]
            if p + 1 < nblk:
                nxt = a[base + B : base + 2 * B, :]
                acc = jnp.where(in_lane[:B], 0.0, nxt)
                for j in range(B):
                    acc = acc - jnp.broadcast_to(nxt[:, base + j : base + j + 1], (B, 128)) * r[j : j + 1, :]
                heads[m] = acc
            left = jnp.where(in_lane, jnp.where(in_sub, jnp.where(lane == sub, -1.0, 0.0), a), 0.0)
            parts = []
            if p > 0:
                parts.append(jnp.zeros((base, 128), F32))
            parts.append(r)
            if p + 1 < nblk:
                parts.append(jnp.zeros((128 - base - B, 128), F32))
            right = jnp.concatenate(parts, axis=0) if len(parts) > 1 else r
            ref[...] = jnp.where(in_lane | in_sub, 0.0, a) - mm(left, right)
        yield


def factor(matrices, work, kept):
    count = len(matrices)
    for i in range(count):
        work[0].at[i][...] = matrices[i][0:HALF, 0:HALF]
    yield from invert([work[0].at[i] for i in range(count)])
    for i in range(count):
        corner = matrices[i][0:HALF, HALF:N]
        kept.append(mm(work[0][i], corner))
        work[1].at[i][...] = matrices[i][HALF:N, HALF:N] - mmt(corner, kept[i])
    yield
    yield from invert([work[1].at[i] for i in range(count)])


def apply(kept, index, target, work):
    upper, lower = target[0:HALF, :], target[HALF:N, :]
    lower = mm(work[1][index], lower - mmt(kept, upper))
    upper = mm(work[0][index], upper) - mm(kept, lower)
    return jnp.concatenate([upper, lower], axis=0)


def whole(ref, *lead):
    return jnp.concatenate([ref[(*lead, slice(0, N))], ref[(*lead, slice(N, 2 * N))]], axis=1)


def main_kernel(two_hbm, one_hbm, src_hbm, couple_two_ref, couple_one_ref, top_ref, rest_ref,
                two_ref, one_ref, src_ref, load_sem, g_ref, pair_ref, total_ref, low, high, *scratch):
    loads = [pltpu.make_async_copy(item, ref, load_sem.at[i]) for i, (item, ref) in
             enumerate([(two_hbm, two_ref), (one_hbm, one_ref), (src_hbm, src_ref)])]
    for item in loads:
        item.start()
    barrier = pltpu.get_barrier_semaphore()
    peers = neighbours()
    for peer in peers:
        pl.semaphore_signal(barrier, inc=1, device_id=peer, device_id_type=pl.DeviceIdType.MESH)
    work = (low, high)

    alive = []

    def tick():
        alive[:] = [item for item in alive if next(item, "end") != "end"]

    def keep(pos, block):
        g_ref[pos, pl.ds(0, N), :] = block[:, :HALF]
        g_ref[pos, pl.ds(N, N), :] = block[:, HALF:]

    def begin(pos):
        out_ref, out_pos = (pair_ref, pos) if pos < PAIRED else (total_ref, pos - PAIRED)
        alive.append(stream(pos, g_ref, out_ref, out_pos, *scratch))
        tick()

    loads[0].wait()
    keep(0, dot3t(split(two_ref[...]), split(two_ref[...])))
    pl.semaphore_wait(barrier, len(peers))
    begin(0)
    loads[1].wait()
    keep(1, dot3t(split(two_ref[...]), split(one_ref[...])))
    begin(1)
    loads[2].wait()
    keep(2, dot3t(split(two_ref[...]), split(src_ref[...])))
    begin(2)
    keep(3, dot3t(split(one_ref[...]), split(one_ref[...])))
    begin(3)
    keep(4, dot3t(split(one_ref[...]), split(src_ref[...])))
    begin(4)
    for _ in range(PHASES - STREAMS):
        tick()
    matrices = [couple_two_ref[h] + whole(pair_ref, 0, h) for h in range(2)]
    kept, left = [], STREAMS - 1
    for step, _ in enumerate(factor(matrices, work, kept)):
        if left and step % 3 == 2:
            tick()
            left -= 1
    for _ in range(left):
        tick()
    half = lax.axis_index("group") // 2
    crosses, solved = [], []
    for h in range(2):
        crosses.append(whole(pair_ref, 1, h))
        solved.append(apply(kept[h], h, jnp.concatenate([crosses[h], whole(pair_ref, 2, h)], axis=1), work))
    lower = jnp.concatenate([whole(total_ref, 0) + couple_one_ref[...], whole(total_ref, 1)], axis=1)
    for h in range(2):
        lower = lower - mmt(crosses[h], solved[h])
    kept = []
    for _ in factor([lower[:, :N]], work, kept):
        pass
    weights = apply(kept[0], 0, lower[:, N:], work)
    mine = jnp.where(half == 0, solved[0], solved[1])
    field = mine[:, N:] - mm(mine[:, :N], weights)
    for pos, item in enumerate([mine[:, :N], field, weights]):
        top, rest = split(item)
        top_ref[:, pos * N : (pos + 1) * N] = top
        rest_ref[:, pos * N : (pos + 1) * N] = rest
    while alive:
        tick()


def main_call(q_two, q_one, sources, couple_two, couple_one):
    vmem = pl.BlockSpec(memory_space=pltpu.VMEM)
    far = pl.BlockSpec(memory_space=pl.ANY)
    shape = jax.ShapeDtypeStruct((N, 3 * N), jnp.bfloat16)
    rows = q_two.shape[0]
    return pl.pallas_call(
        main_kernel,
        in_specs=[far, far, far, vmem, vmem],
        out_specs=[vmem, vmem],
        out_shape=[shape, shape],
        scratch_shapes=[
            pltpu.VMEM((rows, N), F32),
            pltpu.VMEM((rows, N), F32),
            pltpu.VMEM((rows, N), F32),
            pltpu.SemaphoreType.DMA((3,)),
            pltpu.VMEM((STREAMS, 2 * N, HALF), F32),
            pltpu.VMEM((PAIRED, 2, 2 * N, HALF), F32),
            pltpu.VMEM((STREAMS - PAIRED, 2 * N, HALF), F32),
            pltpu.VMEM((2, HALF, HALF), F32),
            pltpu.VMEM((2, HALF, HALF), F32),
            pltpu.VMEM((STREAMS, 256, HALF), F32),
            pltpu.VMEM((STREAMS, 2, 2, 32, HALF), F32),
            pltpu.VMEM((STREAMS, 2, 32, HALF), F32),
            pltpu.VMEM((STREAMS, 2, 32, HALF), F32),
            pltpu.VMEM((STREAMS, NZ - 1, 8, HALF), F32),
            pltpu.VMEM((STREAMS, NY, 8, HALF), F32),
            pltpu.VMEM((STREAMS, 256, HALF), F32),
            pltpu.VMEM((STREAMS, 64, HALF), F32),
            pltpu.VMEM((STREAMS, 8, HALF), F32),
            pltpu.SemaphoreType.DMA((STREAMS, COPIES)),
            pltpu.SemaphoreType.DMA((STREAMS, COPIES)),
        ],
        compiler_params=pltpu.CompilerParams(collective_id=0, has_side_effects=True),
    )(q_two, q_one, sources, couple_two, couple_one)


def update_kernel(two_ref, one_ref, src_ref, top_ref, rest_ref, panel_ref, sol_ref):
    two, one = split(two_ref[...]), split(one_ref[...])
    top, rest = top_ref[...], rest_ref[...]
    wide = dot3(two, (top[:, : 2 * N], rest[:, : 2 * N]))
    panel_ref[...] = one_ref[...] - wide[:, :N]
    sol_ref[...] = src_ref[...] - wide[:, N:] - dot3(one, (top[:, 2 * N :], rest[:, 2 * N :]))


def update_call(q_two, q_one, sources, top, rest, tile):
    rows = q_two.shape[0]
    spec = pl.BlockSpec((tile, N), lambda i: (i, 0))
    full = pl.BlockSpec((N, 3 * N), lambda i: (0, 0))
    shape = jax.ShapeDtypeStruct((rows, N), F32)
    return pl.pallas_call(
        update_kernel,
        grid=(rows // tile,),
        in_specs=[spec, spec, spec, full, full],
        out_specs=[spec, spec],
        out_shape=[shape, shape],
    )(q_two, q_one, sources, top, rest)


def per_device(q_two, q_one, sources, coupling_two, coupling_one):
    top, rest = main_call(q_two, q_one, sources, coupling_two, coupling_one)
    panel_one, result = update_call(q_two, q_one, sources, top, rest, 256)
    return (panel_one, result)


def solution(mesh):
    placed = (
        P(("group", "leaf"), None),
        P(("group", "leaf"), None),
        P(("group", "leaf"), None),
        P(),
        P(),
    )
    return jax.shard_map(
        per_device,
        mesh=mesh,
        in_specs=placed,
        out_specs=(P(("group", "leaf"), None), P(("group", "leaf"), None)),
        check_vma=False,
    )
```

time: 104 us -> 90.5 us (0.87)
  Pallas kernels: 103 us -> 89.6 us
    pallas_call x3 -> x1, Pallas kernels: 94.7 us -> 81.1 us  [main_call(): pl.pallas_call(main_kernel, in_specs=[far, far, far, vmem, vmem], out_spe...]
where the time goes in v2:
time: 90.5 us; the launch traced here: 90.2 us
  Pallas kernels  89.6 us (99%)
    pallas_call x1, Pallas kernels, main_call(): pl.pallas_call(main_kernel, in_specs=[far, far, far, vmem, vmem], out_spe...  81.1 us
    pallas_call x1, Pallas kernels, update_call(): pl.pallas_call(update_kernel, grid=(rows // tile,), in_specs=[spec, spec,...  8.51 us

profile of v2, /device:TPU:1, one launch (start us, length us, event | category | flops | bytes accessed | tf_op | source)
XLA Modules:
  0.0 90.2 jit_solution(14412870637131699590)
XLA Ops:
  0.6 81.1 %shard_map.68 = (bf16[256,768]{1,0:T(8,128)(2,1)}, bf16[256,768]{1,0:T(8,128)(2,1)}) custom-call(f32[2048,256]{1,0:T(8,128)} %two_ref.1, f32[2048,256]{1,0:T(8,128)} %one_ref.1, f32[2048,256]{1,0:T(8,128)} %src_ref.1, f32[2,256,256]{2,1,0:T(8,128)} %couple_two_ref.1, f32[256,256]{1,0:T(8,128)} %couple_one_ref.1), custom_call_target="tpu_custom_call" | custom-call | tf_op jit(solution)/shard_map/pallas_call | solution.py:312
  81.7 8.5 %shard_map.69 = (f32[2048,256]{1,0:T(8,128)}, f32[2048,256]{1,0:T(8,128)}) custom-call(f32[2048,256]{1,0:T(8,128)} %two_ref.1, f32[2048,256]{1,0:T(8,128)} %one_ref.1, f32[2048,256]{1,0:T(8,128)} %src_ref.1, bf16[256,768]{1,0:T(8,128)(2,1)} %get-tuple-element.4.top_ref, bf16[256,768]{1,0:T(8,128)(2,1)} %get-tuple-element.5.rest_ref), custom_call_target="tpu_custom_call" | custom-call | tf_op jit(solution)/shard_map/pallas_call | solution.py:356

commit v3 on v2

--- a/solution.py
+++ b/solution.py
@@ -11,9 +11,10 @@
 N = 256
 HALF = 128
 NC, NX, NZ, NY = 2, 4, 8, 4
-PAIRED = 3
-STREAMS = 5
-PHASES = 10
+PAIRED = 2
+STREAMS = 4
+FLATS = ((0, 128), (128, 256))
+FLAT_COPIES = 1 + (NZ - 1) + (NX * NY - 1) + (NZ - 1) + 1
 COPIES = 1 + 4 + 2 + (NZ - 1) + (NY - 1) + (NZ - 1) + 2 + 2 + 1
 
 
@@ -47,10 +48,129 @@
 
 def neighbours():
     core, x, z, y = here()
-    found = [place(1 - core, x, z, y), place(core, x + 1 - 2 * (x % 2), z, y), place(core, 3 - x, z, y)]
+    found = [place(1 - core, x, z, y)]
     found += [place(core, x, (z + d) % NZ, y) for d in range(1, NZ)]
-    found += [place(core, x, z, (y + d) % NY) for d in range(1, NY)]
+    found += [place(core, (x + d % NX) % NX, z, (y + d // NX) % NY) for d in range(1, NX * NY)]
     return found
+
+
+def flat(pos, g_ref, out_ref, core_buf, z_buf, side_buf, a1, a2, send, recv):
+    base, rows = FLATS[pos]
+    per_core, per_z = rows // NC, rows // NC // NZ
+    core, x, z, y = here()
+    started = []
+    count = [0]
+
+    def copy(src, dst, peer):
+        slot = count[0]
+        count[0] += 1
+        item = pltpu.make_async_remote_copy(
+            src_ref=src, dst_ref=dst, send_sem=send.at[pos, slot], recv_sem=recv.at[pos, slot],
+            device_id=peer, device_id_type=pl.DeviceIdType.MESH)
+        item.start()
+        started.append(item)
+        return item
+
+    mate = place(1 - core, x, z, y)
+    mine = pl.ds(0, per_core)
+    tile = pl.ds(0, per_z)
+    first = copy(g_ref.at[pl.ds(base + (1 - core) * per_core, per_core), :], core_buf.at[pos, mine, :], mate)
+    yield
+    first.wait_recv()
+    a1[pos, mine, :] = g_ref[pl.ds(base + core * per_core, per_core), :] + core_buf[pos, mine, :]
+    wave = []
+    for d in range(1, NZ):
+        to = (z + d) % NZ
+        wave.append(copy(a1.at[pos, pl.ds(to * per_z, per_z), :], z_buf.at[pos, d - 1, tile, :], place(core, x, to, y)))
+    yield
+    for item in wave:
+        item.wait_recv()
+    total = a1[pos, pl.ds(z * per_z, per_z), :]
+    for d in range(1, NZ):
+        total = total + z_buf[pos, d - 1, tile, :]
+    a2[pos, tile, :] = total
+    wave = []
+    for d in range(1, NX * NY):
+        to_x, to_y = (x + d % NX) % NX, (y + d // NX) % NY
+        wave.append(copy(a2.at[pos, tile, :], side_buf.at[pos, d, tile, :], place(core, to_x, z, to_y)))
+    yield
+    for item in wave:
+        item.wait_recv()
+    sums = []
+    for back in range(NY):
+        part = None
+        for d in range(back * NX, back * NX + NX):
+            item = a2[pos, tile, :] if d == 0 else side_buf[pos, d, tile, :]
+            part = item if part is None else part + item
+        sums.append(part)
+    spot = base + core * per_core + z * per_z
+    own = sums[0] + jnp.where(y % 2 == 1, sums[1], sums[3])
+    other = sums[2] + jnp.where(y % 2 == 1, sums[3], sums[1])
+    out_ref[0, pl.ds(spot, per_z), :] = jnp.where(y // 2 == 0, own, other)
+    out_ref[1, pl.ds(spot, per_z), :] = jnp.where(y // 2 == 0, other, own)
+    wave = []
+    for d in range(1, NZ):
+        to = (z + d) % NZ
+        view = out_ref.at[:, pl.ds(spot, per_z), :]
+        wave.append(copy(view, view, place(core, x, to, y)))
+    yield
+    for item in wave:
+        item.wait_recv()
+    view = out_ref.at[:, pl.ds(base + core * per_core, per_core), :]
+    last = copy(view, view, mate)
+    yield
+    last.wait_recv()
+    yield
+    for item in started:
+        item.wait_send()
+
+
+FLAT_LOAD = (("core", 32), ("z", 4), ("xy", 4), ("z", 8), ("core", 64))
+WIDE_LOAD = (("core", 128), ("x", 32), ("x", 16), ("z", 4), ("y", 4), ("z", 4), ("x", 32), ("x", 16), ("core", 128))
+LINK = {"core": (0.0082, 0.9), "x": (0.0215, 1.7), "z": (0.215, 3.3), "y": (0.06, 2.5), "xy": (0.26, 4.0)}
+
+
+def plan(tasks, jobs):
+    loads = []
+    for pos in range(len(FLATS)):
+        loads.append([(name, size * (1 + pos)) for name, size in FLAT_LOAD])
+    for pos in range(STREAMS):
+        scale = [1] * 5 + [2 if pos < PAIRED else 1] * 4
+        loads.append([(name, size * k) for (name, size), k in zip(WIDE_LOAD, scale)])
+    free, due, phase, order = {}, {}, [0] * len(loads), []
+    now, jobs_left = 0.0, jobs
+    todo = list(tasks)
+    while todo or due or jobs_left:
+        ready = [item for item in due if due[item] <= now]
+        if ready:
+            item = min(ready, key=lambda k: (k > 1, due[k]))
+            del due[item]
+            order.append(("serve", item))
+            now += 0.25
+            phase[item] += 1
+        elif todo:
+            kind, item, cost = todo.pop(0)
+            order.append((kind, item))
+            now += cost
+            if kind != "start":
+                continue
+            phase[item] = 0
+        elif jobs_left and phase[0] == len(loads[0]) and (jobs_left > jobs - 8 or phase[1] == len(loads[1])):
+            order.append(("job", 0))
+            jobs_left -= 1
+            now += 0.45
+            continue
+        else:
+            now = min(due.values())
+            continue
+        if phase[item] < len(loads[item]):
+            name, size = loads[item][phase[item]]
+            rate, delay = LINK[name]
+            lane = name[0]
+            begin = max(now, free.get(lane, 0.0))
+            free[lane] = begin + rate * size
+            due[item] = free[lane] + delay
+    return order
 
 
 def stream(pos, g_ref, out_ref, out_pos, core_buf, x_buf, mid_buf, last_buf, z_buf, y_buf, a1, a2, a3, send, recv):
@@ -208,15 +328,15 @@
         yield
 
 
-def factor(matrices, work, kept):
+def factor(matrices, work, kept, right):
     count = len(matrices)
     for i in range(count):
-        work[0].at[i][...] = matrices[i][0:HALF, 0:HALF]
+        work[0].at[i][...] = matrices[i][0]
     yield from invert([work[0].at[i] for i in range(count)])
     for i in range(count):
-        corner = matrices[i][0:HALF, HALF:N]
+        corner = right(i, 0)
         kept.append(mm(work[0][i], corner))
-        work[1].at[i][...] = matrices[i][HALF:N, HALF:N] - mmt(corner, kept[i])
+        work[1].at[i][...] = right(i, 1) - mmt(corner, kept[i])
     yield
     yield from invert([work[1].at[i] for i in range(count)])
 
@@ -233,7 +353,7 @@
 
 
 def main_kernel(two_hbm, one_hbm, src_hbm, couple_two_ref, couple_one_ref, top_ref, rest_ref,
-                two_ref, one_ref, src_ref, load_sem, g_ref, pair_ref, total_ref, low, high, *scratch):
+                two_ref, one_ref, src_ref, load_sem, k_ref, g_ref, base_ref, pair_ref, total_ref, low, high, *scratch):
     loads = [pltpu.make_async_copy(item, ref, load_sem.at[i]) for i, (item, ref) in
              enumerate([(two_hbm, two_ref), (one_hbm, one_ref), (src_hbm, src_ref)])]
     for item in loads:
@@ -243,55 +363,55 @@
     for peer in peers:
         pl.semaphore_signal(barrier, inc=1, device_id=peer, device_id_type=pl.DeviceIdType.MESH)
     work = (low, high)
-
-    alive = []
-
-    def tick():
-        alive[:] = [item for item in alive if next(item, "end") != "end"]
+    flats = len(FLATS)
+    lines = [flat(pos, k_ref, base_ref, *scratch[:7]) for pos in range(flats)]
+    for pos in range(STREAMS):
+        out_ref, out_pos = (pair_ref, pos) if pos < PAIRED else (total_ref, pos - PAIRED)
+        lines.append(stream(pos, g_ref, out_ref, out_pos, *scratch[7:]))
+    factors = [(two_ref, one_ref), (two_ref, src_ref), (one_ref, one_ref), (one_ref, src_ref)]
 
     def keep(pos, block):
         g_ref[pos, pl.ds(0, N), :] = block[:, :HALF]
         g_ref[pos, pl.ds(N, N), :] = block[:, HALF:]
 
-    def begin(pos):
-        out_ref, out_pos = (pair_ref, pos) if pos < PAIRED else (total_ref, pos - PAIRED)
-        alive.append(stream(pos, g_ref, out_ref, out_pos, *scratch))
-        tick()
-
     loads[0].wait()
-    keep(0, dot3t(split(two_ref[...]), split(two_ref[...])))
+    first = dot3t(split(two_ref[...]), split(two_ref[...]))
+    k_ref[0:HALF, :] = first[:HALF, :HALF]
+    k_ref[HALF : HALF + N, :] = first[:, HALF:]
     pl.semaphore_wait(barrier, len(peers))
-    begin(0)
-    loads[1].wait()
-    keep(1, dot3t(split(two_ref[...]), split(one_ref[...])))
-    begin(1)
-    loads[2].wait()
-    keep(2, dot3t(split(two_ref[...]), split(src_ref[...])))
-    begin(2)
-    keep(3, dot3t(split(one_ref[...]), split(one_ref[...])))
-    begin(3)
-    keep(4, dot3t(split(one_ref[...]), split(src_ref[...])))
-    begin(4)
-    for _ in range(PHASES - STREAMS):
-        tick()
-    matrices = [couple_two_ref[h] + whole(pair_ref, 0, h) for h in range(2)]
-    kept, left = [], STREAMS - 1
-    for step, _ in enumerate(factor(matrices, work, kept)):
-        if left and step % 3 == 2:
-            tick()
-            left -= 1
-    for _ in range(left):
-        tick()
+    kept, jobs = [], None
+    tasks = [("start", 0, 0.1), ("start", 1, 0.1)]
+    for pos in range(STREAMS):
+        tasks += [("gram", pos, 0.9), ("start", flats + pos, 0.1)]
+
+    def level_two():
+        matrices = [[couple_two_ref[h, 0:HALF, 0:HALF] + base_ref[h, 0:HALF, :]] for h in range(2)]
+        yield from factor(matrices, work, kept, lambda h, part: couple_two_ref[
+            h, part * HALF : (part + 1) * HALF, HALF:N] + base_ref[h, (part + 1) * HALF : (part + 2) * HALF, :])
+
+    jobs = level_two()
+    for kind, item in plan(tasks, 17):
+        if kind == "gram":
+            if item < 2:
+                loads[item + 1].wait()
+            keep(item, dot3t(split(factors[item][0][...]), split(factors[item][1][...])))
+        elif kind == "job":
+            next(jobs)
+        else:
+            next(lines[item])
+    for _ in jobs:
+        raise RuntimeError("jobs left")
     half = lax.axis_index("group") // 2
     crosses, solved = [], []
     for h in range(2):
-        crosses.append(whole(pair_ref, 1, h))
-        solved.append(apply(kept[h], h, jnp.concatenate([crosses[h], whole(pair_ref, 2, h)], axis=1), work))
+        crosses.append(whole(pair_ref, 0, h))
+        solved.append(apply(kept[h], h, jnp.concatenate([crosses[h], whole(pair_ref, 1, h)], axis=1), work))
     lower = jnp.concatenate([whole(total_ref, 0) + couple_one_ref[...], whole(total_ref, 1)], axis=1)
     for h in range(2):
         lower = lower - mmt(crosses[h], solved[h])
     kept = []
-    for _ in factor([lower[:, :N]], work, kept):
+    for _ in factor([[lower[:HALF, :HALF]]], work, kept,
+                    lambda _, part: lower[part * HALF : (part + 1) * HALF, HALF:N]):
         pass
     weights = apply(kept[0], 0, lower[:, N:], work)
     mine = jnp.where(half == 0, solved[0], solved[1])
@@ -300,8 +420,9 @@
         top, rest = split(item)
         top_ref[:, pos * N : (pos + 1) * N] = top
         rest_ref[:, pos * N : (pos + 1) * N] = rest
-    while alive:
-        tick()
+    for item in lines:
+        for _ in item:
+            raise RuntimeError("stream left")
 
 
 def main_call(q_two, q_one, sources, couple_two, couple_one):
@@ -319,11 +440,20 @@
             pltpu.VMEM((rows, N), F32),
             pltpu.VMEM((rows, N), F32),
             pltpu.SemaphoreType.DMA((3,)),
+            pltpu.VMEM((HALF + N, HALF), F32),
             pltpu.VMEM((STREAMS, 2 * N, HALF), F32),
+            pltpu.VMEM((2, HALF + N, HALF), F32),
             pltpu.VMEM((PAIRED, 2, 2 * N, HALF), F32),
             pltpu.VMEM((STREAMS - PAIRED, 2 * N, HALF), F32),
             pltpu.VMEM((2, HALF, HALF), F32),
             pltpu.VMEM((2, HALF, HALF), F32),
+            pltpu.VMEM((2, 128, HALF), F32),
+            pltpu.VMEM((2, NZ - 1, 16, HALF), F32),
+            pltpu.VMEM((2, NX * NY, 16, HALF), F32),
+            pltpu.VMEM((2, 128, HALF), F32),
+            pltpu.VMEM((2, 16, HALF), F32),
+            pltpu.SemaphoreType.DMA((2, FLAT_COPIES)),
+            pltpu.SemaphoreType.DMA((2, FLAT_COPIES)),
             pltpu.VMEM((STREAMS, 256, HALF), F32),
             pltpu.VMEM((STREAMS, 2, 2, 32, HALF), F32),
             pltpu.VMEM((STREAMS, 2, 32, HALF), F32),
@@ -364,7 +494,7 @@
 
 def per_device(q_two, q_one, sources, coupling_two, coupling_one):
     top, rest = main_call(q_two, q_one, sources, coupling_two, coupling_one)
-    panel_one, result = update_call(q_two, q_one, sources, top, rest, 256)
+    panel_one, result = update_call(q_two, q_one, sources, top, rest, 1024)
     return (panel_one, result)
 
 

time: 90.5 us -> 76 us (0.84)
  Pallas kernels: 89.6 us -> 75.3 us
    pallas_call x1, Pallas kernels: 81.1 us -> 69.1 us  [main_call(): pl.pallas_call(main_kernel, in_specs=[far, far, far, vmem, vmem], out_spe...]
    pallas_call x1, Pallas kernels: 8.51 us -> 6.21 us  [update_call(): pl.pallas_call(update_kernel, grid=(rows // tile,), in_specs=[spec, spec,...]
where the time goes in v3:
time: 76 us; the launch traced here: 75.9 us
  Pallas kernels  75.3 us (99%)
    pallas_call x1, Pallas kernels, main_call(): pl.pallas_call(main_kernel, in_specs=[far, far, far, vmem, vmem], out_spe...  69.1 us
    pallas_call x1, Pallas kernels, update_call(): pl.pallas_call(update_kernel, grid=(rows // tile,), in_specs=[spec, spec,...  6.21 us

profile of v3, /device:TPU:1, one launch (start us, length us, event | category | flops | bytes accessed | tf_op | source)
XLA Modules:
  0.0 75.9 jit_solution(7269366679950974913)
XLA Ops:
  0.6 69.1 %shard_map.68 = (bf16[256,768]{1,0:T(8,128)(2,1)}, bf16[256,768]{1,0:T(8,128)(2,1)}) custom-call(f32[2048,256]{1,0:T(8,128)} %two_ref.1, f32[2048,256]{1,0:T(8,128)} %one_ref.1, f32[2048,256]{1,0:T(8,128)} %src_ref.1, f32[2,256,256]{2,1,0:T(8,128)} %couple_two_ref.1, f32[256,256]{1,0:T(8,128)} %couple_one_ref.1), custom_call_target="tpu_custom_call" | custom-call | tf_op jit(solution)/shard_map/pallas_call | solution.py:433
  69.7 6.2 %shard_map.69 = (f32[2048,256]{1,0:T(8,128)}, f32[2048,256]{1,0:T(8,128)}) custom-call(f32[2048,256]{1,0:T(8,128)} %two_ref.1, f32[2048,256]{1,0:T(8,128)} %one_ref.1, f32[2048,256]{1,0:T(8,128)} %src_ref.1, bf16[256,768]{1,0:T(8,128)(2,1)} %get-tuple-element.4.top_ref, bf16[256,768]{1,0:T(8,128)(2,1)} %get-tuple-element.5.rest_ref), custom_call_target="tpu_custom_call" | custom-call | tf_op jit(solution)/shard_map/pallas_call | solution.py:486

commit v4 on v3

--- a/solution.py
+++ b/solution.py
@@ -13,6 +13,7 @@
 NC, NX, NZ, NY = 2, 4, 8, 4
 PAIRED = 2
 STREAMS = 4
+EARLY, JOBS = 17, 20
 FLATS = ((0, 128), (128, 256))
 FLAT_COPIES = 1 + (NZ - 1) + (NX * NY - 1) + (NZ - 1) + 1
 COPIES = 1 + 4 + 2 + (NZ - 1) + (NY - 1) + (NZ - 1) + 2 + 2 + 1
@@ -128,6 +129,10 @@
 FLAT_LOAD = (("core", 32), ("z", 4), ("xy", 4), ("z", 8), ("core", 64))
 WIDE_LOAD = (("core", 128), ("x", 32), ("x", 16), ("z", 4), ("y", 4), ("z", 4), ("x", 32), ("x", 16), ("core", 128))
 LINK = {"core": (0.0082, 0.9), "x": (0.0215, 1.7), "z": (0.215, 3.3), "y": (0.06, 2.5), "xy": (0.26, 4.0)}
+
+
+def needs(job):
+    return (0,) if job < 8 else (0, 1) if job < EARLY else (0, 1, 2, 3)
 
 
 def plan(tasks, jobs):
@@ -143,7 +148,7 @@
     while todo or due or jobs_left:
         ready = [item for item in due if due[item] <= now]
         if ready:
-            item = min(ready, key=lambda k: (k > 1, due[k]))
+            item = min(ready, key=lambda k: (k > 1, k > 3, due[k]))
             del due[item]
             order.append(("serve", item))
             now += 0.25
@@ -155,10 +160,10 @@
             if kind != "start":
                 continue
             phase[item] = 0
-        elif jobs_left and phase[0] == len(loads[0]) and (jobs_left > jobs - 8 or phase[1] == len(loads[1])):
+        elif jobs_left and all(phase[k] == len(loads[k]) for k in needs(jobs - jobs_left)):
             order.append(("job", 0))
+            now += 0.45 if jobs - jobs_left < EARLY else 0.9
             jobs_left -= 1
-            now += 0.45
             continue
         else:
             now = min(due.values())
@@ -352,16 +357,20 @@
     return jnp.concatenate([ref[(*lead, slice(0, N))], ref[(*lead, slice(N, 2 * N))]], axis=1)
 
 
-def main_kernel(two_hbm, one_hbm, src_hbm, couple_two_ref, couple_one_ref, top_ref, rest_ref,
-                two_ref, one_ref, src_ref, load_sem, k_ref, g_ref, base_ref, pair_ref, total_ref, low, high, *scratch):
-    loads = [pltpu.make_async_copy(item, ref, load_sem.at[i]) for i, (item, ref) in
-             enumerate([(two_hbm, two_ref), (one_hbm, one_ref), (src_hbm, src_ref)])]
-    for item in loads:
-        item.start()
+def main_kernel(two_hbm, one_hbm, src_hbm, couple_two_hbm, couple_one_hbm, top_ref, rest_ref,
+                two_ref, one_ref, src_ref, couple_two_ref, couple_one_ref, load_sem, k_ref, g_ref, base_ref, pair_ref, total_ref, low, high, *scratch):
     barrier = pltpu.get_barrier_semaphore()
     peers = neighbours()
+    piece = two_ref.shape[0] // 4
+    firsts = [pltpu.make_async_copy(two_hbm.at[pl.ds(i * piece, piece), :], two_ref.at[pl.ds(i * piece, piece), :],
+                                    load_sem.at[i]) for i in range(4)]
+    for item in firsts:
+        item.start()
     for peer in peers:
         pl.semaphore_signal(barrier, inc=1, device_id=peer, device_id_type=pl.DeviceIdType.MESH)
+    loads = [pltpu.make_async_copy(item, ref, load_sem.at[4 + i]) for i, (item, ref) in
+             enumerate([(one_hbm, one_ref), (src_hbm, src_ref), (couple_two_hbm, couple_two_ref),
+                        (couple_one_hbm, couple_one_ref)])]
     work = (low, high)
     flats = len(FLATS)
     lines = [flat(pos, k_ref, base_ref, *scratch[:7]) for pos in range(flats)]
@@ -374,26 +383,39 @@
         g_ref[pos, pl.ds(0, N), :] = block[:, :HALF]
         g_ref[pos, pl.ds(N, N), :] = block[:, HALF:]
 
-    loads[0].wait()
+    for item in firsts:
+        item.wait()
+    for item in loads:
+        item.start()
     first = dot3t(split(two_ref[...]), split(two_ref[...]))
     k_ref[0:HALF, :] = first[:HALF, :HALF]
     k_ref[HALF : HALF + N, :] = first[:, HALF:]
     pl.semaphore_wait(barrier, len(peers))
-    kept, jobs = [], None
+    kept = []
     tasks = [("start", 0, 0.1), ("start", 1, 0.1)]
     for pos in range(STREAMS):
         tasks += [("gram", pos, 0.9), ("start", flats + pos, 0.1)]
 
+    crosses, solved, schur = [], [], []
+
     def level_two():
+        for item in loads[2:]:
+            item.wait()
         matrices = [[couple_two_ref[h, 0:HALF, 0:HALF] + base_ref[h, 0:HALF, :]] for h in range(2)]
         yield from factor(matrices, work, kept, lambda h, part: couple_two_ref[
             h, part * HALF : (part + 1) * HALF, HALF:N] + base_ref[h, (part + 1) * HALF : (part + 2) * HALF, :])
+        for h in range(2):
+            crosses.append(whole(pair_ref, 0, h))
+            solved.append(apply(kept[h], h, jnp.concatenate([crosses[h], whole(pair_ref, 1, h)], axis=1), work))
+            yield
+        schur.append(mmt(crosses[0], solved[0]) + mmt(crosses[1], solved[1]))
+        yield
 
     jobs = level_two()
-    for kind, item in plan(tasks, 17):
+    for kind, item in plan(tasks, JOBS):
         if kind == "gram":
             if item < 2:
-                loads[item + 1].wait()
+                loads[item].wait()
             keep(item, dot3t(split(factors[item][0][...]), split(factors[item][1][...])))
         elif kind == "job":
             next(jobs)
@@ -402,13 +424,7 @@
     for _ in jobs:
         raise RuntimeError("jobs left")
     half = lax.axis_index("group") // 2
-    crosses, solved = [], []
-    for h in range(2):
-        crosses.append(whole(pair_ref, 0, h))
-        solved.append(apply(kept[h], h, jnp.concatenate([crosses[h], whole(pair_ref, 1, h)], axis=1), work))
-    lower = jnp.concatenate([whole(total_ref, 0) + couple_one_ref[...], whole(total_ref, 1)], axis=1)
-    for h in range(2):
-        lower = lower - mmt(crosses[h], solved[h])
+    lower = jnp.concatenate([whole(total_ref, 0) + couple_one_ref[...], whole(total_ref, 1)], axis=1) - schur[0]
     kept = []
     for _ in factor([[lower[:HALF, :HALF]]], work, kept,
                     lambda _, part: lower[part * HALF : (part + 1) * HALF, HALF:N]):
@@ -432,14 +448,16 @@
     rows = q_two.shape[0]
     return pl.pallas_call(
         main_kernel,
-        in_specs=[far, far, far, vmem, vmem],
+        in_specs=[far] * 5,
         out_specs=[vmem, vmem],
         out_shape=[shape, shape],
         scratch_shapes=[
             pltpu.VMEM((rows, N), F32),
             pltpu.VMEM((rows, N), F32),
             pltpu.VMEM((rows, N), F32),
-            pltpu.SemaphoreType.DMA((3,)),
+            pltpu.VMEM((2, N, N), F32),
+            pltpu.VMEM((N, N), F32),
+            pltpu.SemaphoreType.DMA((8,)),
             pltpu.VMEM((HALF + N, HALF), F32),
             pltpu.VMEM((STREAMS, 2 * N, HALF), F32),
             pltpu.VMEM((2, HALF + N, HALF), F32),

time: 76 us -> 73 us (0.961)
  Pallas kernels: 75.3 us -> 72.3 us
    pallas_call x1, Pallas kernels: 69.1 us -> 66 us  [main_call(): pl.pallas_call(main_kernel, in_specs=[far] * 5, out_specs=[vmem, vmem], o...]
where the time goes in v4:
time: 73 us; the launch traced here: 72.9 us
  Pallas kernels  72.3 us (99%)
    pallas_call x1, Pallas kernels, main_call(): pl.pallas_call(main_kernel, in_specs=[far] * 5, out_specs=[vmem, vmem], o...  66 us
    pallas_call x1, Pallas kernels, update_call(): pl.pallas_call(update_kernel, grid=(rows // tile,), in_specs=[spec, spec,...  6.21 us

profile of v4, /device:TPU:1, one launch (start us, length us, event | category | flops | bytes accessed | tf_op | source)
XLA Modules:
  0.0 72.9 jit_solution(14125234949965854572)
XLA Ops:
  0.6 66.0 %shard_map.68 = (bf16[256,768]{1,0:T(8,128)(2,1)}, bf16[256,768]{1,0:T(8,128)(2,1)}) custom-call(f32[2048,256]{1,0:T(8,128)} %two_ref.1, f32[2048,256]{1,0:T(8,128)} %one_ref.1, f32[2048,256]{1,0:T(8,128)} %src_ref.1, f32[2,256,256]{2,1,0:T(8,128)} %couple_two_hbm.1, f32[256,256]{1,0:T(8,128)} %couple_one_hbm.1), custom_call_target="tpu_custom_call" | custom-call | tf_op jit(solution)/shard_map/pallas_call | solution.py:449
  66.7 6.2 %shard_map.69 = (f32[2048,256]{1,0:T(8,128)}, f32[2048,256]{1,0:T(8,128)}) custom-call(f32[2048,256]{1,0:T(8,128)} %two_ref.1, f32[2048,256]{1,0:T(8,128)} %one_ref.1, f32[2048,256]{1,0:T(8,128)} %src_ref.1, bf16[256,768]{1,0:T(8,128)(2,1)} %get-tuple-element.4.top_ref, bf16[256,768]{1,0:T(8,128)(2,1)} %get-tuple-element.5.rest_ref), custom_call_target="tpu_custom_call" | custom-call | tf_op jit(solution)/shard_map/pallas_call | solution.py:504

commit v5 on v4

--- a/solution.py
+++ b/solution.py
@@ -13,7 +13,7 @@
 NC, NX, NZ, NY = 2, 4, 8, 4
 PAIRED = 2
 STREAMS = 4
-EARLY, JOBS = 17, 20
+EARLY, JOBS, SIDE = 17, 37, 3
 FLATS = ((0, 128), (128, 256))
 FLAT_COPIES = 1 + (NZ - 1) + (NX * NY - 1) + (NZ - 1) + 1
 COPIES = 1 + 4 + 2 + (NZ - 1) + (NY - 1) + (NZ - 1) + 2 + 2 + 1
@@ -132,20 +132,20 @@
 
 
 def needs(job):
-    return (0,) if job < 8 else (0, 1) if job < EARLY else (0, 1, 2, 3)
-
-
-def plan(tasks, jobs):
+    return (0,) if job < 8 else (0, 1) if job < EARLY else (0, 1, 2) if job < EARLY + 2 else (0, 1, 2, 3)
+
+
+def plan(tasks, jobs, sides):
     loads = []
     for pos in range(len(FLATS)):
         loads.append([(name, size * (1 + pos)) for name, size in FLAT_LOAD])
     for pos in range(STREAMS):
-        scale = [1] * 5 + [2 if pos < PAIRED else 1] * 4
+        scale = [1] * 5 + [2 - pos % 2] * 4
         loads.append([(name, size * k) for (name, size), k in zip(WIDE_LOAD, scale)])
     free, due, phase, order = {}, {}, [0] * len(loads), []
-    now, jobs_left = 0.0, jobs
+    now, jobs_left, side = 0.0, jobs, 0
     todo = list(tasks)
-    while todo or due or jobs_left:
+    while todo or due or jobs_left or side < sides:
         ready = [item for item in due if due[item] <= now]
         if ready:
             item = min(ready, key=lambda k: (k > 1, k > 3, due[k]))
@@ -162,8 +162,14 @@
             phase[item] = 0
         elif jobs_left and all(phase[k] == len(loads[k]) for k in needs(jobs - jobs_left)):
             order.append(("job", 0))
-            now += 0.45 if jobs - jobs_left < EARLY else 0.9
+            now += 0.45
             jobs_left -= 1
+            continue
+        elif side < sides and jobs - jobs_left >= EARLY + 2 and all(
+                phase[k] == len(loads[k]) for k in ((4,) if side < 2 else (4, 5))):
+            order.append(("side", 0))
+            now += 0.6
+            side += 1
             continue
         else:
             now = min(due.values())
@@ -180,7 +186,7 @@
 
 def stream(pos, g_ref, out_ref, out_pos, core_buf, x_buf, mid_buf, last_buf, z_buf, y_buf, a1, a2, a3, send, recv):
     core, x, z, y = here()
-    paired = pos < PAIRED
+    paired = pos % 2 == 0
     near, far, across = x + 1 - 2 * (x % 2), 3 - x, (x + 2) % NX
     started = []
     count = [0]
@@ -348,8 +354,9 @@
 
 def apply(kept, index, target, work):
     upper, lower = target[0:HALF, :], target[HALF:N, :]
-    lower = mm(work[1][index], lower - mmt(kept, upper))
-    upper = mm(work[0][index], upper) - mm(kept, lower)
+    parts, head = split(kept), split(upper)
+    lower = dot3(split(work[1][index]), split(lower - dot3t(parts, head)))
+    upper = dot3(split(work[0][index]), head) - dot3(parts, split(lower))
     return jnp.concatenate([upper, lower], axis=0)
 
 
@@ -375,9 +382,9 @@
     flats = len(FLATS)
     lines = [flat(pos, k_ref, base_ref, *scratch[:7]) for pos in range(flats)]
     for pos in range(STREAMS):
-        out_ref, out_pos = (pair_ref, pos) if pos < PAIRED else (total_ref, pos - PAIRED)
+        out_ref, out_pos = (pair_ref if pos % 2 == 0 else total_ref, pos // 2)
         lines.append(stream(pos, g_ref, out_ref, out_pos, *scratch[7:]))
-    factors = [(two_ref, one_ref), (two_ref, src_ref), (one_ref, one_ref), (one_ref, src_ref)]
+    factors = [(two_ref, one_ref), (one_ref, one_ref), (two_ref, src_ref), (one_ref, src_ref)]
 
     def keep(pos, block):
         g_ref[pos, pl.ds(0, N), :] = block[:, :HALF]
@@ -396,7 +403,8 @@
     for pos in range(STREAMS):
         tasks += [("gram", pos, 0.9), ("start", flats + pos, 0.1)]
 
-    crosses, solved, schur = [], [], []
+    crosses, solved, fields, top, targets = [], [], [], [], []
+    last = (low.at[pl.ds(2, 1)], high.at[pl.ds(2, 1)])
 
     def level_two():
         for item in loads[2:]:
@@ -406,35 +414,47 @@
             h, part * HALF : (part + 1) * HALF, HALF:N] + base_ref[h, (part + 1) * HALF : (part + 2) * HALF, :])
         for h in range(2):
             crosses.append(whole(pair_ref, 0, h))
-            solved.append(apply(kept[h], h, jnp.concatenate([crosses[h], whole(pair_ref, 1, h)], axis=1), work))
+            solved.append(apply(kept[h], h, crosses[h], work))
             yield
-        schur.append(mmt(crosses[0], solved[0]) + mmt(crosses[1], solved[1]))
+        root = whole(total_ref, 0) + couple_one_ref[...]
+        for h in range(2):
+            root = root - dot3t(split(crosses[h]), split(solved[h]))
         yield
-
+        yield from factor([[root[:HALF, :HALF]]], last, top, lambda _, part: root[
+            part * HALF : (part + 1) * HALF, HALF:N])
+
+    def right_side():
+        for h in range(2):
+            fields.append(apply(kept[h], h, whole(pair_ref, 1, h), work))
+            yield
+        value = whole(total_ref, 1)
+        for h in range(2):
+            value = value - dot3t(split(crosses[h]), split(fields[h]))
+        targets.append(value)
+        yield
+
+    side = right_side()
     jobs = level_two()
-    for kind, item in plan(tasks, JOBS):
+    for kind, item in plan(tasks, JOBS, SIDE):
         if kind == "gram":
-            if item < 2:
-                loads[item].wait()
+            if item % 2 == 0:
+                loads[item // 2].wait()
             keep(item, dot3t(split(factors[item][0][...]), split(factors[item][1][...])))
         elif kind == "job":
             next(jobs)
+        elif kind == "side":
+            next(side)
         else:
             next(lines[item])
     for _ in jobs:
         raise RuntimeError("jobs left")
     half = lax.axis_index("group") // 2
-    lower = jnp.concatenate([whole(total_ref, 0) + couple_one_ref[...], whole(total_ref, 1)], axis=1) - schur[0]
-    kept = []
-    for _ in factor([[lower[:HALF, :HALF]]], work, kept,
-                    lambda _, part: lower[part * HALF : (part + 1) * HALF, HALF:N]):
-        pass
-    weights = apply(kept[0], 0, lower[:, N:], work)
+    weights = apply(top[0], 0, targets[0], last)
     mine = jnp.where(half == 0, solved[0], solved[1])
-    field = mine[:, N:] - mm(mine[:, :N], weights)
-    for pos, item in enumerate([mine[:, :N], field, weights]):
-        top, rest = split(item)
-        top_ref[:, pos * N : (pos + 1) * N] = top
+    field = jnp.where(half == 0, fields[0], fields[1]) - dot3(split(mine), split(weights))
+    for pos, item in enumerate([mine, field, weights]):
+        lead, rest = split(item)
+        top_ref[:, pos * N : (pos + 1) * N] = lead
         rest_ref[:, pos * N : (pos + 1) * N] = rest
     for item in lines:
         for _ in item:
@@ -463,8 +483,8 @@
             pltpu.VMEM((2, HALF + N, HALF), F32),
             pltpu.VMEM((PAIRED, 2, 2 * N, HALF), F32),
             pltpu.VMEM((STREAMS - PAIRED, 2 * N, HALF), F32),
-            pltpu.VMEM((2, HALF, HALF), F32),
-            pltpu.VMEM((2, HALF, HALF), F32),
+            pltpu.VMEM((3, HALF, HALF), F32),
+            pltpu.VMEM((3, HALF, HALF), F32),
             pltpu.VMEM((2, 128, HALF), F32),
             pltpu.VMEM((2, NZ - 1, 16, HALF), F32),
             pltpu.VMEM((2, NX * NY, 16, HALF), F32),

time: 73 us -> 71.3 us (0.977)
  Pallas kernels: 72.3 us -> 70.2 us
    pallas_call x1, Pallas kernels: 66 us -> 64 us  [main_call(): pl.pallas_call(main_kernel, in_specs=[far] * 5, out_specs=[vmem, vmem], o...]
where the time goes in v5:
time: 71.3 us; the launch traced here: 70.9 us
  Pallas kernels  70.2 us (98%)
    pallas_call x1, Pallas kernels, main_call(): pl.pallas_call(main_kernel, in_specs=[far] * 5, out_specs=[vmem, vmem], o...  64 us
    pallas_call x1, Pallas kernels, update_call(): pl.pallas_call(update_kernel, grid=(rows // tile,), in_specs=[spec, spec,...  6.22 us

profile of v5, /device:TPU:1, one launch (start us, length us, event | category | flops | bytes accessed | tf_op | source)
XLA Modules:
  0.0 70.9 jit_solution(3428664330181871745)
XLA Ops:
  0.6 64.0 %shard_map.68 = (bf16[256,768]{1,0:T(8,128)(2,1)}, bf16[256,768]{1,0:T(8,128)(2,1)}) custom-call(f32[2048,256]{1,0:T(8,128)} %two_ref.1, f32[2048,256]{1,0:T(8,128)} %one_ref.1, f32[2048,256]{1,0:T(8,128)} %src_ref.1, f32[2,256,256]{2,1,0:T(8,128)} %couple_two_hbm.1, f32[256,256]{1,0:T(8,128)} %couple_one_hbm.1), custom_call_target="tpu_custom_call" | custom-call | tf_op jit(solution)/shard_map/pallas_call | solution.py:469
  64.7 6.2 %shard_map.69 = (f32[2048,256]{1,0:T(8,128)}, f32[2048,256]{1,0:T(8,128)}) custom-call(f32[2048,256]{1,0:T(8,128)} %two_ref.1, f32[2048,256]{1,0:T(8,128)} %one_ref.1, f32[2048,256]{1,0:T(8,128)} %src_ref.1, bf16[256,768]{1,0:T(8,128)(2,1)} %get-tuple-element.4.top_ref, bf16[256,768]{1,0:T(8,128)(2,1)} %get-tuple-element.5.rest_ref), custom_call_target="tpu_custom_call" | custom-call | tf_op jit(solution)/shard_map/pallas_call | solution.py:524
